TPU v7x, 32 devices: a whole 2x2x4 slice. The times are simulated.
32 devices in a mesh: seq: 4 (over y, x), exp: 8 (over z, core).
Axes of the slice: x: 2, y: 2, z: 4, core: 2. Of those that a mesh axis runs over, the one named last changes fastest.
Arguments:
- inputs: bfloat16 [4096, 4096], P(('seq', 'exp')), may hold values from -6 to 6
- queries: bfloat16 [4096, 4096], P(('seq', 'exp')), may hold values from -40 to 40
- keys: bfloat16 [4096, 4096], P(('seq', 'exp')), may hold values from -4 to 4
- values: bfloat16 [4096, 4096], P(('seq', 'exp')), may hold values from -6 to 6
- norm_gain: float32 [4096], replicated, may hold values from 0.25 to 1.75
- expert_ids: int32 [4096, 2], P(('seq', 'exp')), may hold values from 0 to 7, all different within a row; in each aligned block of 128 rows (0 to 127, 128 to 255, ...) at most 32 rows name the same one
- gate_weights: float32 [4096, 2], P(('seq', 'exp')), may hold values from 0.2 to 1
- pairs: int32 [16, 2], replicated, may hold values from 0 to 7, as said below
- w_gate: bfloat16 [8, 4096, 4096], P('exp', None, 'seq'), may hold values from -0.09375 to 0.09375
- w_up: bfloat16 [8, 4096, 4096], P('exp', None, 'seq'), may hold values from -0.09375 to 0.09375
- w_down: bfloat16 [8, 4096, 4096], P('exp', 'seq'), may hold values from -0.09375 to 0.09375
Outputs:
- output: bfloat16 [4096, 4096], P(('seq', 'exp'))
Inputs may be any that keep to these rules, and one draw needn't show every extreme that they name: `pairs`: each row is (query block, key block) with the key block from the query block - 2 to the query block; rows are distinct; every block is paired with itself; some pair has distance 2. `expert_ids`: the 2 ids of a token differ; within the 128 rows of one device every expert is named exactly 32 times.
All inputs are finite; a program needn't handle non-finite values.
Results may differ from a plain program's by a relative error of at most 0.007.
Values may be sent and summed in bfloat16 or wider, within the bound.
A program may use at most 128 MiB of HBM per device.

v0:
```python
import functools
import math

import jax
import jax.numpy as jnp
from jax import lax
from jax.experimental import pallas as pl
from jax.experimental.pallas import tpu as pltpu
from jax.sharding import PartitionSpec as P

HSZ = 128
TOP = 2
BLK = 512
DIST = 2
OUTER = 2

very_negative = -1e30
norm_epsilon = 1e-05

MESH = pl.DeviceIdType.MESH
ANY = pl.BlockSpec(memory_space=pl.ANY)
DMA = pltpu.SemaphoreType.DMA


def remote(source, target, send_sem, recv_sem, device):
    return pltpu.make_async_remote_copy(
        src_ref=source,
        dst_ref=target,
        send_sem=send_sem,
        recv_sem=recv_sem,
        device_id=device,
        device_id_type=MESH,
    )


def enter(peers):
    barrier = pltpu.get_barrier_semaphore()
    for peer in peers:
        pl.semaphore_signal(barrier, inc=1, device_id=peer, device_id_type=MESH)
    pl.semaphore_wait(barrier, len(peers))


def turned(index, steps, count):
    return lax.rem(index + (steps % count), count)


def params(collective_id, vmem=None):
    return pltpu.CompilerParams(
        collective_id=collective_id, has_side_effects=True, vmem_limit_bytes=vmem
    )


def qkv_kernel(
    seq_count, exp_count, tail, q_ref, k_ref, v_ref, qr_ref, kx_ref, vx_ref,
    local_sem, z_send, z_recv, f_send, f_recv,
):
    s, e = lax.axis_index("seq"), lax.axis_index("exp")
    rows = q_ref.shape[0]
    group = qr_ref.shape[1]
    run = qr_ref.shape[0]
    arrays = ((k_ref, kx_ref, tail), (v_ref, vx_ref, tail), (q_ref, qr_ref, 0))
    enter(
        [(s, turned(e, k, exp_count)) for k in range(1, exp_count)]
        + [(turned(s, 1, seq_count), e), (turned(s, -1, seq_count), e)]
    )

    def columns(ref, index):
        return ref.at[:, pl.ds(pl.multiple_of(index * group, group), group)]

    def lines(ref, offset, index):
        return ref.at[pl.ds(pl.multiple_of(offset + index * rows, rows), rows)]

    waits = []
    for i, (source, target, offset) in enumerate(arrays):
        for k in range(1, exp_count):
            d = turned(e, k, exp_count)
            copy = remote(
                columns(source, d), lines(target, offset, e), z_send.at[i, k], z_recv.at[i, k], (s, d)
            )
            copy.start()
            waits.append(copy)
    locals_ = []
    for i, (source, target, offset) in enumerate(arrays):
        copy = pltpu.make_async_copy(columns(source, e), lines(target, offset, e), local_sem.at[i])
        copy.start()
        locals_.append(copy)

    def relay(i, k, act):
        source, target, offset = arrays[i]
        c = turned(e, -k, exp_count)
        inside = (c + 1) * rows > run - tail
        block = columns(source, e) if k == 0 else lines(target, offset, c)
        row = pl.multiple_of(lax.max(c * rows - (run - tail), 0), rows)
        copy = remote(
            block, target.at[pl.ds(row, rows)], f_send.at[i, k], f_recv.at[i, k],
            (turned(s, 1, seq_count), e),
        )
        if act == "start":
            pl.when(inside & (s < seq_count - 1))(copy.start)
        elif act == "send":
            pl.when(inside & (s < seq_count - 1))(copy.wait_send)
        else:
            pl.when(inside & (s > 0))(copy.wait_recv)

    for i in range(3):
        for k in range(exp_count):
            if k > 0:
                source, target, offset = arrays[i]
                block = lines(target, offset, turned(e, -k, exp_count))
                remote(block, block, z_send.at[i, k], z_recv.at[i, k], (s, e)).wait_recv()
            if i < 2:
                relay(i, k, "start")
    for i in range(2):
        for k in range(exp_count):
            relay(i, k, "recv")
            relay(i, k, "send")
    for copy in waits:
        copy.wait_send()
    for copy in locals_:
        copy.wait()


def exchange_qkv(queries, keys, values, seq_count, exp_count, tail):
    rows, width = queries.shape
    group, run = width // exp_count, rows * exp_count
    kind = queries.dtype
    return pl.pallas_call(
        functools.partial(qkv_kernel, seq_count, exp_count, tail),
        out_shape=(
            jax.ShapeDtypeStruct((run, group), kind),
            jax.ShapeDtypeStruct((tail + run, group), kind),
            jax.ShapeDtypeStruct((tail + run, group), kind),
        ),
        in_specs=[ANY] * 3,
        out_specs=(ANY,) * 3,
        scratch_shapes=[
            DMA((3,)),
            DMA((3, exp_count)),
            DMA((3, exp_count)),
            DMA((2, exp_count)),
            DMA((2, exp_count)),
        ],
        compiler_params=params(1),
        name="qkv_exchange",
    )(queries, keys, values)


def attend_kernel(
    seq_count, exp_count, slots, present_ref, q_ref, k_ref, v_ref, o_ref, att_ref, local_sem, z_send, z_recv
):
    s, e = lax.axis_index("seq"), lax.axis_index("exp")
    rows = o_ref.shape[0]
    run, group = q_ref.shape
    heads, blocks, owners = group // HSZ, run // BLK, BLK // rows
    scale = 1.0 / math.sqrt(HSZ)
    enter([(s, turned(e, k, exp_count)) for k in range(1, exp_count)])

    def source(owner, head):
        return att_ref.at[
            pl.ds(pl.multiple_of(owner * rows, rows), rows), pl.ds(pl.multiple_of(head * HSZ, HSZ), HSZ)
        ]

    def target(giver, head):
        return o_ref.at[:, pl.ds(pl.multiple_of(giver * group + head * HSZ, HSZ), HSZ)]

    def send(owner, head):
        return remote(
            source(owner, head), target(e, head), z_send.at[owner, head], z_recv.at[e, head], (s, owner)
        )

    def own(head):
        return pltpu.make_async_copy(source(e, head), target(e, head), local_sem.at[head])

    def step(i, carry):
        head = lax.rem(i, heads)
        block = lax.rem(lax.div(e, owners) + 1 + lax.div(i, heads), blocks)
        column = pl.ds(pl.multiple_of(head * HSZ, HSZ), HSZ)

        def lines(slot):
            return pl.ds(pl.multiple_of((block + slot) * BLK, BLK), BLK)

        q = q_ref[lines(0), column]
        scores = []
        for j in range(slots):
            score = lax.dot_general(
                q, k_ref[lines(j), column], (((1,), (1,)), ((), ())), preferred_element_type=jnp.float32
            )
            scores.append(jnp.where(present_ref[block, j] > 0, score * scale, very_negative))
        top = functools.reduce(jnp.maximum, [jnp.max(x, axis=1, keepdims=True) for x in scores])
        total, summed = 0.0, 0.0
        for j in range(slots):
            exps = jnp.exp(scores[j] - top)
            total = total + jnp.sum(exps, axis=1, keepdims=True)
            value = v_ref[lines(j), column]
            value = jnp.where(present_ref[block, j] > 0, value, jnp.zeros_like(value))
            summed = summed + jnp.dot(
                exps.astype(jnp.bfloat16), value, preferred_element_type=jnp.float32
            )
        att_ref[lines(0), column] = (summed / total).astype(att_ref.dtype)
        for j in range(owners):
            owner = block * owners + j

            @pl.when(owner != e)
            def _():
                send(owner, head).start()

            @pl.when(owner == e)
            def _():
                own(head).start()

        return carry

    lax.fori_loop(0, blocks * heads, step, 0)
    for head in range(heads):
        for k in range(1, exp_count):
            giver, owner = turned(e, -k, exp_count), turned(e, k, exp_count)
            block = target(giver, head)
            remote(block, block, z_send.at[giver, head], z_recv.at[giver, head], (s, e)).wait_recv()
            send(owner, head).wait_send()
        own(head).wait()


def attend(query_run, keys_ext, values_ext, present, seq_count, exp_count):
    run, group = query_run.shape
    heads = group // HSZ
    held = pl.BlockSpec(memory_space=pltpu.VMEM)
    return pl.pallas_call(
        functools.partial(attend_kernel, seq_count, exp_count, present.shape[1]),
        out_shape=jax.ShapeDtypeStruct((run // exp_count, group * exp_count), query_run.dtype),
        in_specs=[pl.BlockSpec(memory_space=pltpu.SMEM)] + [held] * 3,
        out_specs=ANY,
        scratch_shapes=[
            pltpu.VMEM((run, group), query_run.dtype),
            DMA((heads,)),
            DMA((exp_count, heads)),
            DMA((exp_count, heads)),
        ],
        compiler_params=params(2, 48 * 1024 * 1024),
        name="attend",
    )(present, query_run, keys_ext, values_ext)


def experts_kernel(
    seq_count, exp_count, together, tile, wide_tile,
    out_ref, gate_hbm, up_hbm, down_hbm, got_ref,
    gate_ref, up_ref, down_ref, buf, x_ref, hid_ref, in0, in1, out0, out1, mid0, mid1, done,
    local_sem, w_sem, z_send, z_recv, x_send, x_recv, d_send, d_recv,
    p_send, p_recv, m_send, m_recv, g_send, g_recv,
):
    s, e = lax.axis_index("seq"), lax.axis_index("exp")
    inner_count = seq_count // OUTER
    capacity, width = out_ref.shape[1:]
    half = width // 2
    a, b = lax.div(s, inner_count), lax.rem(s, inner_count)
    other = 1 - a
    outer = (other * inner_count + b, e)
    steps = range(1, inner_count)
    forth = [turned(b, j, inner_count) for j in steps]
    back = [turned(b, -j, inner_count) for j in steps]
    inner = [(a * inner_count + f, e) for f in forth]
    low, high = pl.ds(0, half), pl.ds(half, half)
    groups = exp_count // together
    chunk_rows = seq_count * capacity

    def chunk(k):
        return lax.rem(e - k + exp_count, exp_count)

    def arrived(block, send_sem, recv_sem):
        remote(block, block, send_sem, recv_sem, (s, e)).wait_recv()

    weights = [
        pltpu.make_async_copy(source.at[0], target, w_sem.at[i])
        for i, (source, target) in enumerate(
            ((gate_hbm, gate_ref), (up_hbm, up_ref), (down_hbm, down_ref))
        )
    ]
    own = pltpu.make_async_copy(out_ref.at[e], buf.at[a, b, e], local_sem)
    own.start()
    enter([(s, turned(e, k, exp_count)) for k in range(1, exp_count)] + [outer] + inner)

    def spread(k):
        d = lax.rem(e + k, exp_count)
        return remote(out_ref.at[d], buf.at[a, b, e], z_send.at[k], z_recv.at[k], (s, d))

    def directs(k):
        block = buf.at[a, b, chunk(k)]
        return [
            remote(block, block, x_send.at[i, k], x_recv.at[i, k], peer)
            for i, peer in enumerate([outer] + inner)
        ]

    def relays(k):
        c = chunk(k)
        copies = []
        for j, peer in enumerate(inner):
            block = buf.at[other, b, c, :, low]
            copies.append(remote(block, block, d_send.at[0, j, k], d_recv.at[0, j, k], peer))
            block = buf.at[a, back[j], c, :, high]
            copies.append(remote(block, block, d_send.at[1, j, k], d_recv.at[1, j, k], outer))
        return copies

    def gather_step(k):
        @pl.when(k < exp_count)
        def _():
            @pl.when(k > 0)
            def _():
                arrived(buf.at[a, b, chunk(k)], z_send.at[k], z_recv.at[k])

            for copy in directs(k):
                copy.start()

        @pl.when((k > 0) & (k <= exp_count))
        def _():
            n = k - 1
            c = chunk(n)
            arrived(buf.at[other, b, c], x_send.at[0, n], x_recv.at[0, n])
            for j in range(inner_count - 1):
                arrived(buf.at[a, back[j], c], x_send.at[1 + j, n], x_recv.at[1 + j, n])
            for copy in relays(n):
                copy.start()

    def complete(k):
        c = chunk(k)
        for j in range(inner_count - 1):
            for h, part in enumerate((low, high)):
                arrived(buf.at[other, back[j], c, :, part], d_send.at[h, j, k], d_recv.at[h, j, k])

    def first(k):
        c = chunk(k)
        return [
            remote(buf.at[other, :, c, :, high], in1.at[k], p_send.at[0, k], p_recv.at[0, k], outer)
        ] + [
            remote(
                buf.at[:, f, c, :, low], in0.at[j, k], p_send.at[1 + j, k], p_recv.at[1 + j, k], inner[j]
            )
            for j, f in enumerate(forth)
        ]

    def second(k):
        return [remote(out0.at[k], mid0.at[k], m_send.at[0, k], m_recv.at[0, k], outer)] + [
            remote(out1.at[j, k], mid1.at[j, k], m_send.at[1 + j, k], m_recv.at[1 + j, k], inner[j])
            for j in range(inner_count - 1)
        ]

    def third(k):
        return remote(done.at[k], got_ref.at[e], g_send.at[k], g_recv.at[k], (s, chunk(k)))

    def stay():
        return pltpu.make_async_copy(done.at[0], got_ref.at[e], local_sem)

    def wide(value):
        return value.astype(jnp.float32)

    def inner_sum(k, side):
        total = wide(buf[side, b, chunk(k), :, low])
        for j in range(inner_count - 1):
            total = total + wide(in0[j, k, side])
        return total

    def outer_sum(k, lane):
        return wide(buf[a, lane, chunk(k), :, high]) + wide(in1[k, lane])

    def sum_step(k):
        @pl.when((k >= 0) & (k < exp_count))
        def _():
            sends = second(k)
            for j in range(inner_count - 1):
                arrived(in0.at[j, k], p_send.at[1 + j, k], p_recv.at[1 + j, k])
            out0[k] = inner_sum(k, other).astype(out0.dtype)
            sends[0].start()
            arrived(in1.at[k], p_send.at[0, k], p_recv.at[0, k])
            for j, f in enumerate(forth):
                out1[j, k] = outer_sum(k, f).astype(out1.dtype)
                sends[1 + j].start()

        @pl.when((k > 0) & (k <= exp_count))
        def _():
            n = k - 1
            arrived(mid0.at[n], m_send.at[0, n], m_recv.at[0, n])
            done[n, :, low] = (inner_sum(n, a) + wide(mid0[n])).astype(done.dtype)
            total = outer_sum(n, b)
            for j in range(inner_count - 1):
                arrived(mid1.at[j, n], m_send.at[1 + j, n], m_recv.at[1 + j, n])
                total = total + wide(mid1[j, n])
            done[n, :, high] = total.astype(done.dtype)

            @pl.when(n == 0)
            def _():
                stay().start()

            @pl.when(n > 0)
            def _():
                third(n).start()

    def loop(begin, end, body):
        def step(i, carry):
            body(i)
            return carry

        lax.fori_loop(begin, end, step, 0)

    loop(1, exp_count, lambda k: spread(k).start())
    own.wait()
    for copy in weights:
        copy.start()
    loop(0, together + 2, gather_step)
    for copy in weights:
        copy.wait()
    tiles, wide_tiles = hid_ref.shape[1] // tile, width // wide_tile
    stride, wide_stride = max(1, tiles // together), max(1, wide_tiles // together)

    def group(p):
        base = p * together
        for i in range(together):
            complete(base + i)
            x_ref[pl.ds(i * chunk_rows, chunk_rows)] = buf[:, :, chunk(base + i)].reshape(chunk_rows, width)

        def hidden_tile(n):
            where = pl.ds(pl.multiple_of(n * tile, tile), tile)
            x = x_ref[...]
            gate = jnp.dot(x, gate_ref[:, where], preferred_element_type=jnp.float32)
            up = jnp.dot(x, up_ref[:, where], preferred_element_type=jnp.float32)
            hid_ref[:, where] = (jax.nn.silu(gate) * up).astype(hid_ref.dtype)

            @pl.when(lax.rem(n, stride) == 0)
            def _():
                gather_step(base + together + 2 + lax.div(n, stride))

        loop(0, tiles, hidden_tile)
        for i in range(together):
            for copy in directs(base + i) + relays(base + i):
                copy.wait_send()

        def down_tile(n):
            where = pl.ds(pl.multiple_of(n * wide_tile, wide_tile), wide_tile)
            y = jnp.dot(hid_ref[...], down_ref[:, where], preferred_element_type=jnp.float32).astype(buf.dtype)
            for i in range(together):
                buf[:, :, chunk(base + i), :, where] = y[i * chunk_rows : (i + 1) * chunk_rows].reshape(
                    OUTER, inner_count, capacity, wide_tile
                )

            @pl.when(lax.rem(n, wide_stride) == 0)
            def _():
                sum_step(base - together + lax.div(n, wide_stride))

        loop(0, wide_tiles, down_tile)
        for i in range(together):
            for copy in first(base + i):
                copy.start()

    loop(0, groups, group)
    loop((groups - 1) * together, exp_count + 1, sum_step)

    def finish(k):
        for copy in first(k) + second(k):
            copy.wait_send()

        @pl.when(k > 0)
        def _():
            spread(k).wait_send()
            third(k).wait_send()
            arrived(got_ref.at[lax.rem(e + k, exp_count)], g_send.at[k], g_recv.at[k])

    loop(0, exp_count, finish)
    stay().wait()


def experts(outgoing, w_gate, w_up, w_down, seq_count, exp_count):
    exp_count, capacity, width = outgoing.shape
    hidden = w_gate.shape[2]
    inner_count = seq_count // OUTER
    inner_peers = inner_count - 1
    half = width // 2
    kind = outgoing.dtype
    together = 1
    while 2 * together * seq_count * capacity <= 256 and exp_count % (2 * together) == 0:
        together *= 2
    rows = together * seq_count * capacity
    tile, wide_tile = min(256, hidden // together), min(512, width // together)
    vmem = [
        w_gate.shape[1:],
        w_up.shape[1:],
        w_down.shape[1:],
        (OUTER, inner_count, exp_count, capacity, width),
        (rows, width),
        (rows, hidden),
        (inner_peers, exp_count, OUTER, capacity, half),
        (exp_count, inner_count, capacity, half),
        (exp_count, capacity, half),
        (inner_peers, exp_count, capacity, half),
        (exp_count, capacity, half),
        (inner_peers, exp_count, capacity, half),
        (exp_count, capacity, width),
    ]
    one, per_peer, per_side = (exp_count,), (inner_count, exp_count), (2, inner_peers, exp_count)
    sems = [one, one, per_peer, per_peer, per_side, per_side, per_peer, per_peer, per_peer, per_peer, one, one]
    return pl.pallas_call(
        functools.partial(experts_kernel, seq_count, exp_count, together, tile, wide_tile),
        out_shape=jax.ShapeDtypeStruct((exp_count, capacity, width), kind),
        in_specs=[ANY] * 4,
        out_specs=ANY,
        scratch_shapes=[pltpu.VMEM(shape, kind) for shape in vmem]
        + [DMA, DMA((3,))]
        + [DMA(shape) for shape in sems],
        compiler_params=params(3, 60 * 1024 * 1024),
        name="experts",
    )(outgoing, w_gate, w_up, w_down)


def per_device(
    inputs, queries, keys, values, norm_gain, expert_ids, gate_weights, pairs, w_gate, w_up, w_down
):
    rows_dev, model_width = inputs.shape
    seq_count, exp_count = lax.axis_size("seq"), lax.axis_size("exp")
    query_run, keys_ext, values_ext = exchange_qkv(
        queries, keys, values, seq_count, exp_count, DIST * BLK
    )
    blocks_dev = query_run.shape[0] // BLK
    query_block = lax.axis_index("seq") * blocks_dev + jnp.arange(blocks_dev, dtype=jnp.int32)
    key_block = query_block[:, None] - (DIST - jnp.arange(DIST + 1, dtype=jnp.int32))[None, :]
    present = jnp.any(
        (pairs[None, None, :, 0] == query_block[:, None, None])
        & (pairs[None, None, :, 1] == key_block[:, :, None]),
        axis=2,
    ).astype(jnp.int32)
    attended = attend(query_run, keys_ext, values_ext, present, seq_count, exp_count)
    mixed_sum = inputs.astype(jnp.float32) + attended.astype(jnp.float32)
    mean_square = jnp.mean(mixed_sum * mixed_sum, axis=1, keepdims=True)
    normed = (mixed_sum * lax.rsqrt(mean_square + norm_epsilon) * norm_gain[None, :]).astype(
        jnp.bfloat16
    )
    capacity = rows_dev * TOP // exp_count
    places = exp_count * capacity
    flat_ids = expert_ids.reshape(-1)
    id_table = (flat_ids[:, None] == jnp.arange(exp_count, dtype=jnp.int32)[None, :]).astype(
        jnp.int32
    )
    ahead_count = jnp.cumsum(id_table, axis=0) - id_table
    position = jnp.sum(ahead_count * id_table, axis=1)
    target = (flat_ids * capacity + position).reshape(rows_dev, TOP)
    slots = jnp.arange(places, dtype=jnp.int32)
    spots = target[:, :, None] == slots[None, None, :]
    choose = jnp.any(spots, axis=1).astype(jnp.bfloat16)
    outgoing = (
        lax.dot_general(choose, normed, (((0,), (0,)), ((), ())), preferred_element_type=jnp.float32)
        .astype(jnp.bfloat16)
        .reshape(exp_count, capacity, model_width)
    )
    got = experts(outgoing, w_gate, w_up, w_down, seq_count, exp_count)
    weight = jnp.sum(jnp.where(spots, gate_weights[:, :, None], 0.0), axis=1)
    coarse = weight.astype(jnp.bfloat16)
    fine = (weight - coarse.astype(jnp.float32)).astype(jnp.bfloat16)
    flat = got.reshape(places, model_width)
    combined = jnp.dot(coarse, flat, preferred_element_type=jnp.float32) + jnp.dot(
        fine, flat, preferred_element_type=jnp.float32
    )
    return (mixed_sum + combined).astype(jnp.bfloat16)


def solution(mesh):
    rows = P(("seq", "exp"), None)
    in_specs = (
        rows, rows, rows, rows, P(), rows, rows, P(),
        P("exp", None, "seq"), P("exp", None, "seq"), P("exp", "seq", None),
    )
    return jax.shard_map(
        per_device, mesh=mesh, in_specs=in_specs, out_specs=rows, check_vma=False
    )
```

profile of v0, /device:TPU:25, one launch (start us, length us, event | category | flops | bytes accessed | tf_op | source)
XLA Modules:
  0.0 280.5 jit_solution(15362279719797539780)
XLA Ops:
  0.0 0.8 slice_bitcast_fusion.1
  0.8 0.1 broadcast_compare_fusion
  0.8 0.1 broadcast_subtract_fusion
  0.9 0.2 and_reduce_fusion
  1.1 72.5 %qkv_exchange.1 = (bf16[1024,512]{1,0:T(8,128)(2,1)}, bf16[2048,512]{1,0:T(8,128)(2,1)}, bf16[2048,512]{1,0:T(8,128)(2,1)}) custom-call(bf16[128,4096]{1,0:T(8,128)(2,1)} %q_ref.1, bf16[128,4096]{1,0:T(8,128)(2,1)} %k_ref.1, bf16[128,4096]{1,0:T(8,128)(2,1)} %v_ref.1), custom_call_target="tpu_custom_call" | custom-call | tf_op jit(solution)/shard_map/qkv_exchange/pallas_call | solution.py:127
  73.7 0.0 copy-start
  73.7 1.6 copy-done
  75.3 1.2 copy-done.1
  76.5 30.3 %attend.1 = bf16[128,4096]{1,0:T(8,128)(2,1)S(1)} custom-call(s32[2,3]{1,0:T(2,128)S(1)} %convert_element_type.36.present_ref, bf16[1024,512]{1,0:T(8,128)(2,1)S(1)} %copy-done.1, bf16[2048,512]{1,0:T(8,128)(2,1)S(1)} %copy-done, bf16[2048,512]{1,0:T(8,128)(2,1)} %get-tuple-element.10.v_ref), custom_call_target="tpu_custom_call" | custom-call | tf_op jit(solution)/shard_map/attend/pallas_call | solution.py:227
  106.8 0.0 copy-done.3
  106.8 0.0 copy-start.5
  106.8 0.0 copy-start.4
  106.8 0.4 multiply_reduce_fusion
  107.3 0.2 copy-done.5
  107.5 0.1 copy.24
  107.6 0.1 eq.85
  107.8 0.6 reduce-window.6
  108.3 0.2 slice_reduce_fusion
  108.6 0.1 eq.81
  108.8 0.1 fusion.9
  108.8 0.1 reduce_sum.30
  109.0 0.1 copy.26
  109.1 0.1 fusion.4
  109.2 0.0 copy-done.4
  109.2 2.2 convolution_convert_fusion
  111.4 164.9 %experts.1 = bf16[8,32,4096]{2,1,0:T(8,128)(2,1)} custom-call(bf16[8,32,4096]{2,1,0:T(8,128)(2,1)} %bitcast.19, bf16[1,4096,1024]{2,1,0:T(8,128)(2,1)} %gate_hbm.1, bf16[1,4096,1024]{2,1,0:T(8,128)(2,1)} %up_hbm.1, bf16[1,1024,4096]{2,1,0:T(8,128)(2,1)} %down_hbm.1), custom_call_target="tpu_custom_call" | custom-call | tf_op jit(solution)/shard_map/experts/pallas_call | solution.py:497
  276.3 0.0 copy-done.6
  276.3 0.1 select_reduce_fusion
  276.5 0.0 copy-start.2
  276.5 2.2 fusion.6
  278.7 0.0 copy-done.2
  278.7 1.8 fusion.1
  (11 shorter events, 0.1 us)
Async XLA Ops:
  73.7 1.6 copy-start
  75.3 1.2 copy-start.1
  76.5 30.3 %copy-start.3 = (bf16[128,4096]{1,0:T(8,128)(2,1)S(1)}, bf16[128,4096]{1,0:T(8,128)(2,1)}, u32[]{:S(2)}) copy-start(bf16[128,4096]{1,0:T(8,128)(2,1)} %param.11) | copy-start | bytes 3145732
  106.8 0.7 copy-start.5
  106.8 2.4 copy-start.4
  111.4 164.9 %copy-start.6 = (f32[128,2]{0,1:T(2,128)S(1)}, f32[128,2]{0,1:T(2,128)}, u32[]{:S(2)}) copy-start(f32[128,2]{0,1:T(2,128)} %param.17) | copy-start | bytes 3076
  276.5 2.2 copy-start.2
where the time goes:
time: 286 us; the launch traced here: 280 us
  Pallas kernels  268 us (94%)
  matrix products  6.15 us (2%)
  local copies, waits for them, and re-layouts  4.63 us (2%)
    pallas_call x1, Pallas kernels, experts(): pl.pallas_call(functools.partial(experts_kernel, seq_count, exp_count, to...  165 us
    pallas_call x1, Pallas kernels, exchange_qkv(): pl.pallas_call(functools.partial(qkv_kernel, seq_count, exp_count, tail),...  72.5 us
    pallas_call x1, Pallas kernels, attend(): pl.pallas_call(functools.partial(attend_kernel, seq_count, exp_count, pre...  30.3 us

commit v1 on v0

v1 whole, which is shorter than its diff:
```python
import functools
import math

import jax
import jax.numpy as jnp
from jax import lax
from jax.experimental import pallas as pl
from jax.experimental.pallas import tpu as pltpu
from jax.sharding import PartitionSpec as P

HSZ = 128
TOP = 2
BLK = 512
DIST = 2
OUTER = 2
CORES = 2

very_negative = -1e30
norm_epsilon = 1e-05

MESH = pl.DeviceIdType.MESH
ANY = pl.BlockSpec(memory_space=pl.ANY)
HELD = pl.BlockSpec(memory_space=pltpu.VMEM)
DMA = pltpu.SemaphoreType.DMA


def remote(source, target, send_sem, recv_sem, device):
    return pltpu.make_async_remote_copy(
        src_ref=source,
        dst_ref=target,
        send_sem=send_sem,
        recv_sem=recv_sem,
        device_id=device,
        device_id_type=MESH,
    )


def turned(index, steps, count):
    return lax.rem(index + (steps % count), count)


def xor(one, two, count):
    total, bit = 0, 1
    while bit < count:
        total = total + bit * lax.rem(lax.div(one, bit) + lax.div(two, bit), 2)
        bit *= 2
    return total


def loop(begin, end, body):
    def step(i, carry):
        body(i)
        return carry

    lax.fori_loop(begin, end, step, 0)


def wide(value):
    return value.astype(jnp.float32)


def layer_kernel(
    seq_count, exp_count, tail, together, tile, wide_tile, norm_tile,
    pairs_ref, ids_ref, gate_weight_ref, gain_ref, in_hbm, q_hbm, k_hbm, v_hbm, gate_hbm, up_hbm, down_hbm,
    out_ref,
    present, x_in, q_run, k_run, v_run, attended, outgoing, got, choose_ref, coarse_ref, fine_ref,
    gate_ref, up_ref, down_ref, buf, x_ref, hid_ref, in0, in1, out0, out1, mid0, mid1, done,
    in_sem, own_sem, q_send, q_recv, f_send, f_recv, a_own, a_send, a_recv,
    local_sem, stay_sem, w_sem, z_send, z_recv, x_send, x_recv, d_send, d_recv,
    p_send, p_recv, m_send, m_recv, g_send, g_recv,
):
    s, e = lax.axis_index("seq"), lax.axis_index("exp")
    z, c = lax.div(e, CORES), lax.rem(e, CORES)
    chips = exp_count // CORES
    rows, width = x_in.shape
    run, group = q_run.shape
    heads, blocks, owners = group // HSZ, run // BLK, BLK // rows
    slots = DIST + 1
    capacity = buf.shape[3]
    inner_count = seq_count // OUTER
    half = width // 2
    a, b = lax.div(s, inner_count), lax.rem(s, inner_count)
    other = 1 - a
    outer = (other * inner_count + b, e)
    steps = range(1, inner_count)
    forth = [turned(b, j, inner_count) for j in steps]
    back = [turned(b, -j, inner_count) for j in steps]
    inner = [(a * inner_count + f, e) for f in forth]
    low, high = pl.ds(0, half), pl.ds(half, half)
    groups = exp_count // together
    chunk_rows = seq_count * capacity

    def arrived(block, send_sem, recv_sem):
        remote(block, block, send_sem, recv_sem, (s, e)).wait_recv()

    def columns(ref, index):
        return ref.at[:, pl.ds(pl.multiple_of(index * group, group), group)]

    def place(index):
        return lax.rem(index, CORES) * chips + lax.div(index, CORES)

    def lines(ref, offset, index):
        return ref.at[pl.ds(pl.multiple_of(offset + index * rows, rows), rows)]

    def landing(i, owner):
        if i == 2:
            return lines(q_run, 0, place(owner))
        return lines((k_run, v_run)[i], tail, owner)

    sources = (k_hbm, v_hbm, q_hbm)

    def give(i, k):
        d = xor(e, k, exp_count)
        return remote(columns(sources[i], d), landing(i, e), q_send.at[i, k], q_recv.at[i, k], (s, d))

    def keep(i):
        return pltpu.make_async_copy(columns(sources[i], e), landing(i, e), own_sem.at[i])

    def taken(i, k):
        block = landing(i, xor(e, k, exp_count))
        arrived(block, q_send.at[i, k], q_recv.at[i, k])

    def relay(i, k, act):
        owner = xor(e, k, exp_count)
        inside = (owner + 1) * rows > run - tail
        row = pl.multiple_of(lax.max(owner * rows - (run - tail), 0), rows)
        copy = remote(
            landing(i, owner), (k_run, v_run)[i].at[pl.ds(row, rows)], f_send.at[i, k], f_recv.at[i, k],
            (turned(s, 1, seq_count), e),
        )
        if act == "start":
            pl.when(inside & (s < seq_count - 1))(copy.start)
        elif act == "send":
            pl.when(inside & (s < seq_count - 1))(copy.wait_send)
        else:
            pl.when(inside & (s > 0))(copy.wait_recv)

    barrier = pltpu.get_barrier_semaphore()
    for k in range(1, exp_count):
        pl.semaphore_signal(barrier, inc=1, device_id=(s, turned(e, k, exp_count)), device_id_type=MESH)
    for k in range(1, seq_count):
        pl.semaphore_signal(barrier, inc=1, device_id=(turned(s, k, seq_count), e), device_id_type=MESH)
    pl.semaphore_wait(barrier, exp_count + seq_count - 2)

    for i in range(2):
        for k in range(1, exp_count):
            give(i, k).start()

    @pl.when(c == 0)
    def _():
        for k in range(1, exp_count):
            give(2, k).start()

    for i in range(3):
        keep(i).start()
    inputs_copy = pltpu.make_async_copy(in_hbm, x_in, in_sem)
    inputs_copy.start()
    weights = [
        pltpu.make_async_copy(source.at[0], target, w_sem.at[i])
        for i, (source, target) in enumerate(
            ((gate_hbm, gate_ref), (up_hbm, up_ref), (down_hbm, down_ref))
        )
    ]
    for copy in weights:
        copy.start()

    first_block = s * blocks
    wanted = [(first_block + i, first_block + i - (DIST - j)) for i in range(blocks) for j in range(slots)]

    def seen(p, found):
        query, key = pairs_ref[p, 0], pairs_ref[p, 1]
        return tuple(
            f + jnp.where((query == w[0]) & (key == w[1]), 1, 0) for f, w in zip(found, wanted)
        )

    found = lax.fori_loop(0, pairs_ref.shape[0], seen, (jnp.int32(0),) * len(wanted))
    for i in range(blocks):
        for j in range(slots):
            present[i, j] = found[i * slots + j]

    places = exp_count * capacity
    named = [ids_ref[:, t : t + 1] for t in range(TOP)]
    ranks = lax.broadcasted_iota(jnp.int32, (rows, HSZ), 1)
    marks = [jnp.where(n == ranks, 1.0, 0.0) for n in named]
    earlier = jnp.where(
        lax.broadcasted_iota(jnp.int32, (rows, rows), 1) < lax.broadcasted_iota(jnp.int32, (rows, rows), 0),
        1.0, 0.0,
    ).astype(jnp.bfloat16)
    ahead = jnp.dot(earlier, sum(marks).astype(jnp.bfloat16), preferred_element_type=jnp.float32)
    slot_ids = lax.broadcasted_iota(jnp.int32, (rows, places), 1)
    choose = jnp.zeros((rows, places), jnp.float32)
    weight = jnp.zeros((rows, places), jnp.float32)
    for t in range(TOP):
        position = jnp.sum(ahead * marks[t], axis=1, keepdims=True)
        spot = named[t] * capacity + position.astype(jnp.int32) == slot_ids
        choose = jnp.where(spot, 1.0, choose)
        weight = jnp.where(spot, gate_weight_ref[:, t : t + 1], weight)
    choose_ref[...] = choose.astype(jnp.bfloat16)
    coarse = weight.astype(jnp.bfloat16)
    coarse_ref[...] = coarse
    fine_ref[...] = (weight - coarse.astype(jnp.float32)).astype(jnp.bfloat16)

    for i in range(2):
        keep(i).wait()
        relay(i, 0, "start")
        for k in range(1, exp_count):
            taken(i, k)
            relay(i, k, "start")
    keep(2).wait()

    def queries_of(parity):
        for j in range(chips):
            k = CORES * j + lax.rem(c + parity, CORES)
            if j == 0:
                pl.when(k > 0)(functools.partial(taken, 2, k))
            else:
                taken(2, k)

    queries_of(0)

    @pl.when(c > 0)
    def _():
        for k in range(1, exp_count):
            give(2, k).start()

    for i in range(2):
        for k in range(exp_count):
            relay(i, k, "recv")

    scale = 1.0 / math.sqrt(HSZ)

    def piece(owner, head):
        return q_run.at[
            pl.ds(pl.multiple_of(place(owner) * rows, rows), rows), pl.ds(pl.multiple_of(head * HSZ, HSZ), HSZ)
        ]

    def goal(giver, head):
        return attended.at[:, pl.ds(pl.multiple_of(giver * group + head * HSZ, HSZ), HSZ)]

    def send(owner, head):
        return remote(
            piece(owner, head), goal(e, head), a_send.at[owner, head], a_recv.at[e, head], (s, owner)
        )

    def own(head):
        return pltpu.make_async_copy(piece(e, head), goal(e, head), a_own.at[head])

    part = BLK // CORES

    def attend(parity):
        def step(i):
            head = lax.rem(i, heads)
            block = lax.rem(lax.div(e, owners) + 1 + lax.div(i, heads), blocks)
            column = pl.ds(pl.multiple_of(head * HSZ, HSZ), HSZ)
            mine = pl.ds(pl.multiple_of(parity * (run // CORES) + block * part, part), part)

            def span(slot):
                return pl.ds(pl.multiple_of((block + slot) * BLK, BLK), BLK)

            q = q_run[mine, column]
            scores = []
            for j in range(slots):
                score = lax.dot_general(
                    q, k_run[span(j), column], (((1,), (1,)), ((), ())), preferred_element_type=jnp.float32
                )
                scores.append(jnp.where(present[block, j] > 0, score * scale, very_negative))
            top = functools.reduce(jnp.maximum, [jnp.max(x, axis=1, keepdims=True) for x in scores])
            total, summed = 0.0, 0.0
            for j in range(slots):
                exps = jnp.exp(scores[j] - top)
                total = total + jnp.sum(exps, axis=1, keepdims=True)
                value = v_run[span(j), column]
                value = jnp.where(present[block, j] > 0, value, jnp.zeros_like(value))
                summed = summed + jnp.dot(
                    exps.astype(jnp.bfloat16), value, preferred_element_type=jnp.float32
                )
            q_run[mine, column] = (summed / total).astype(q_run.dtype)
            for j in range(owners // CORES):
                owner = block * owners + CORES * j + parity

                @pl.when(owner != e)
                def _():
                    send(owner, head).start()

                @pl.when(owner == e)
                def _():
                    own(head).start()

        loop(0, blocks * heads, step)

    def mixed(where):
        return wide(x_in[:, where]) + wide(attended[:, where])

    def chunk(t):
        return CORES * xor(z, lax.rem(t, chips), chips) + lax.div(t, chips)

    def spread(k):
        d = xor(e, k, exp_count)
        step = c * chips + lax.div(k, CORES)
        return remote(outgoing.at[d], buf.at[a, b, e], z_send.at[k], z_recv.at[step], (s, d))

    def stays():
        return pltpu.make_async_copy(outgoing.at[e], buf.at[a, b, e], local_sem)

    def dispatch():
        inputs_copy.wait()

        def squares(k, total):
            giver = xor(e, k, exp_count)

            @pl.when(k > 0)
            def _():
                for head in range(heads):
                    block = goal(giver, head)
                    arrived(block, a_send.at[giver, head], a_recv.at[giver, head])

            @pl.when(k == 0)
            def _():
                for head in range(heads):
                    own(head).wait()

            value = mixed(pl.ds(pl.multiple_of(giver * group, group), group))
            return total + jnp.sum(value * value, axis=1, keepdims=True)

        total = lax.fori_loop(0, exp_count, squares, jnp.zeros((rows, 1), jnp.float32))
        factor = lax.rsqrt(total / width + norm_epsilon)

        def normed_tile(n):
            where = pl.ds(pl.multiple_of(n * norm_tile, norm_tile), norm_tile)
            normed = (mixed(where) * factor * gain_ref[:, where]).astype(jnp.bfloat16)
            picked = lax.dot_general(
                choose_ref[...], normed, (((0,), (0,)), ((), ())), preferred_element_type=jnp.float32
            )
            outgoing[:, :, where] = picked.astype(outgoing.dtype).reshape(exp_count, capacity, norm_tile)

        loop(0, width // norm_tile, normed_tile)
        stays().start()
        loop(1, exp_count, lambda k: spread(k).start())

    attend(0)
    pl.when(c == 0)(dispatch)
    queries_of(1)
    attend(1)
    pl.when(c > 0)(dispatch)

    def directs(k):
        block = buf.at[a, b, chunk(k)]
        return [
            remote(block, block, x_send.at[i, k], x_recv.at[i, k], peer)
            for i, peer in enumerate([outer] + inner)
        ]

    def relays(k):
        n = chunk(k)
        copies = []
        for j, peer in enumerate(inner):
            block = buf.at[other, b, n, :, low]
            copies.append(remote(block, block, d_send.at[0, j, k], d_recv.at[0, j, k], peer))
            block = buf.at[a, back[j], n, :, high]
            copies.append(remote(block, block, d_send.at[1, j, k], d_recv.at[1, j, k], outer))
        return copies

    def gather_step(k):
        @pl.when(k < exp_count)
        def _():
            @pl.when(k != c * chips)
            def _():
                arrived(buf.at[a, b, chunk(k)], z_send.at[k], z_recv.at[k])

            @pl.when(k == c * chips)
            def _():
                stays().wait()

            for copy in directs(k):
                copy.start()

        @pl.when((k > 0) & (k <= exp_count))
        def _():
            n = k - 1
            m = chunk(n)
            arrived(buf.at[other, b, m], x_send.at[0, n], x_recv.at[0, n])
            for j in range(inner_count - 1):
                arrived(buf.at[a, back[j], m], x_send.at[1 + j, n], x_recv.at[1 + j, n])
            for copy in relays(n):
                copy.start()

    def complete(k):
        n = chunk(k)
        for j in range(inner_count - 1):
            for h, side in enumerate((low, high)):
                arrived(buf.at[other, back[j], n, :, side], d_send.at[h, j, k], d_recv.at[h, j, k])

    def first(k):
        n = chunk(k)
        return [
            remote(buf.at[other, :, n, :, high], in1.at[k], p_send.at[0, k], p_recv.at[0, k], outer)
        ] + [
            remote(
                buf.at[:, f, n, :, low], in0.at[j, k], p_send.at[1 + j, k], p_recv.at[1 + j, k], inner[j]
            )
            for j, f in enumerate(forth)
        ]

    def second(k):
        return [remote(out0.at[k], mid0.at[k], m_send.at[0, k], m_recv.at[0, k], outer)] + [
            remote(out1.at[j, k], mid1.at[j, k], m_send.at[1 + j, k], m_recv.at[1 + j, k], inner[j])
            for j in range(inner_count - 1)
        ]

    def third(k):
        d = chunk(k)
        where = xor(e, d, exp_count)
        return remote(done.at[k], got.at[e], g_send.at[k], g_recv.at[where], (s, d))

    def stay():
        return pltpu.make_async_copy(done.at[c * chips], got.at[e], stay_sem)

    def inner_sum(k, side):
        total = wide(buf[side, b, chunk(k), :, low])
        for j in range(inner_count - 1):
            total = total + wide(in0[j, k, side])
        return total

    def outer_sum(k, lane):
        return wide(buf[a, lane, chunk(k), :, high]) + wide(in1[k, lane])

    def sum_step(k):
        @pl.when((k >= 0) & (k < exp_count))
        def _():
            sends = second(k)
            for j in range(inner_count - 1):
                arrived(in0.at[j, k], p_send.at[1 + j, k], p_recv.at[1 + j, k])
            out0[k] = inner_sum(k, other).astype(out0.dtype)
            sends[0].start()
            arrived(in1.at[k], p_send.at[0, k], p_recv.at[0, k])
            for j, f in enumerate(forth):
                out1[j, k] = outer_sum(k, f).astype(out1.dtype)
                sends[1 + j].start()

        @pl.when((k > 0) & (k <= exp_count))
        def _():
            n = k - 1
            arrived(mid0.at[n], m_send.at[0, n], m_recv.at[0, n])
            done[n, :, low] = (inner_sum(n, a) + wide(mid0[n])).astype(done.dtype)
            total = outer_sum(n, b)
            for j in range(inner_count - 1):
                arrived(mid1.at[j, n], m_send.at[1 + j, n], m_recv.at[1 + j, n])
                total = total + wide(mid1[j, n])
            done[n, :, high] = total.astype(done.dtype)

            @pl.when(n == c * chips)
            def _():
                stay().start()

            @pl.when(n != c * chips)
            def _():
                third(n).start()

    loop(0, together + 2, gather_step)
    for copy in weights:
        copy.wait()
    tiles, wide_tiles = hid_ref.shape[1] // tile, width // wide_tile
    stride, wide_stride = max(1, tiles // together), max(1, wide_tiles // together)

    def expert_group(p):
        base = p * together
        for i in range(together):
            complete(base + i)
            x_ref[pl.ds(i * chunk_rows, chunk_rows)] = buf[:, :, chunk(base + i)].reshape(chunk_rows, width)

        def hidden_tile(n):
            where = pl.ds(pl.multiple_of(n * tile, tile), tile)
            x = x_ref[...]
            gate = jnp.dot(x, gate_ref[:, where], preferred_element_type=jnp.float32)
            up = jnp.dot(x, up_ref[:, where], preferred_element_type=jnp.float32)
            hid_ref[:, where] = (jax.nn.silu(gate) * up).astype(hid_ref.dtype)

            @pl.when(lax.rem(n, stride) == 0)
            def _():
                gather_step(base + together + 2 + lax.div(n, stride))

        loop(0, tiles, hidden_tile)
        for i in range(together):
            for copy in directs(base + i) + relays(base + i):
                copy.wait_send()

        def down_tile(n):
            where = pl.ds(pl.multiple_of(n * wide_tile, wide_tile), wide_tile)
            y = jnp.dot(hid_ref[...], down_ref[:, where], preferred_element_type=jnp.float32).astype(buf.dtype)
            for i in range(together):
                buf[:, :, chunk(base + i), :, where] = y[i * chunk_rows : (i + 1) * chunk_rows].reshape(
                    OUTER, inner_count, capacity, wide_tile
                )

            @pl.when(lax.rem(n, wide_stride) == 0)
            def _():
                sum_step(base - together + lax.div(n, wide_stride))

        loop(0, wide_tiles, down_tile)
        for i in range(together):
            for copy in first(base + i):
                copy.start()

    loop(0, groups, expert_group)
    loop((groups - 1) * together, exp_count + 1, sum_step)

    stay().wait()
    for k in range(1, exp_count):
        arrived(got.at[xor(e, k, exp_count)], g_send.at[k], g_recv.at[k])

    def final_tile(n):
        where = pl.ds(pl.multiple_of(n * norm_tile, norm_tile), norm_tile)
        flat = got[:, :, where].reshape(places, norm_tile)
        combined = jnp.dot(coarse_ref[...], flat, preferred_element_type=jnp.float32) + jnp.dot(
            fine_ref[...], flat, preferred_element_type=jnp.float32
        )
        out_ref[:, where] = (mixed(where) + combined).astype(out_ref.dtype)

    loop(0, width // norm_tile, final_tile)

    for i in range(2):
        for k in range(exp_count):
            relay(i, k, "send")
    for i in range(3):
        for k in range(1, exp_count):
            give(i, k).wait_send()

    def finish(k):
        for copy in first(k) + second(k):
            copy.wait_send()

        @pl.when(k > 0)
        def _():
            spread(k).wait_send()
            for head in range(heads):
                send(xor(e, k, exp_count), head).wait_send()

        @pl.when(k != c * chips)
        def _():
            third(k).wait_send()

    loop(0, exp_count, finish)


def per_device(
    inputs, queries, keys, values, norm_gain, expert_ids, gate_weights, pairs, w_gate, w_up, w_down
):
    rows, width = inputs.shape
    seq_count, exp_count = lax.axis_size("seq"), lax.axis_size("exp")
    tail = DIST * BLK
    run, group = rows * exp_count, queries.shape[1] // exp_count
    heads, blocks = group // HSZ, run // BLK
    capacity = rows * TOP // exp_count
    places = exp_count * capacity
    hidden = w_gate.shape[2]
    inner_count = seq_count // OUTER
    inner_peers = inner_count - 1
    half = width // 2
    kind = inputs.dtype
    together = 1
    while 2 * together * seq_count * capacity <= 256 and exp_count % (2 * together) == 0:
        together *= 2
    group_rows = together * seq_count * capacity
    tile, wide_tile, norm_tile = min(256, hidden // together), min(512, width // together), min(512, width)
    vmem = [
        (rows, width),
        (run, group),
        (tail + run, group),
        (tail + run, group),
        (rows, width),
        (exp_count, capacity, width),
        (exp_count, capacity, width),
        (rows, places),
        (rows, places),
        (rows, places),
        w_gate.shape[1:],
        w_up.shape[1:],
        w_down.shape[1:],
        (OUTER, inner_count, exp_count, capacity, width),
        (group_rows, width),
        (group_rows, hidden),
        (inner_peers, exp_count, OUTER, capacity, half),
        (exp_count, inner_count, capacity, half),
        (exp_count, capacity, half),
        (inner_peers, exp_count, capacity, half),
        (exp_count, capacity, half),
        (inner_peers, exp_count, capacity, half),
        (exp_count, capacity, width),
    ]
    one, per_peer, per_side = (exp_count,), (inner_count, exp_count), (2, inner_peers, exp_count)
    sems = [
        (3, exp_count), (3, exp_count), (2, exp_count), (2, exp_count), (heads,), (exp_count, heads),
        (exp_count, heads),
    ]
    more = [one, one, per_peer, per_peer, per_side, per_side, per_peer, per_peer, per_peer, per_peer, one, one]
    return pl.pallas_call(
        functools.partial(layer_kernel, seq_count, exp_count, tail, together, tile, wide_tile, norm_tile),
        out_shape=jax.ShapeDtypeStruct((rows, width), kind),
        in_specs=[pl.BlockSpec(memory_space=pltpu.SMEM)] + [HELD] * 3 + [ANY] * 7,
        out_specs=HELD,
        scratch_shapes=[pltpu.SMEM((blocks, DIST + 1), jnp.int32)]
        + [pltpu.VMEM(shape, kind) for shape in vmem]
        + [DMA, DMA((3,))]
        + [DMA(shape) for shape in sems]
        + [DMA, DMA, DMA((3,))]
        + [DMA(shape) for shape in more],
        compiler_params=pltpu.CompilerParams(
            collective_id=1, has_side_effects=True, vmem_limit_bytes=67043328
        ),
        name="layer",
    )(
        pairs, expert_ids, gate_weights, norm_gain.reshape(1, width), inputs, queries, keys, values,
        w_gate, w_up, w_down,
    )


def solution(mesh):
    rows = P(("seq", "exp"), None)
    in_specs = (
        rows, rows, rows, rows, P(), rows, rows, P(),
        P("exp", None, "seq"), P("exp", None, "seq"), P("exp", "seq", None),
    )
    return jax.shard_map(
        per_device, mesh=mesh, in_specs=in_specs, out_specs=rows, check_vma=False
    )
```

time: 286 us -> 273 us (0.955)
  matrix products: 6.15 us -> 0 us
  Pallas kernels: 268 us -> 262 us
    dot_general x3 -> x0, matrix products: 6.15 us -> none  [the longest x1 2.18 us: per_device(): jnp.dot(coarse, flat, preferred_element_type=jnp.float32)]
    pallas_call x3 -> x1, Pallas kernels: 268 us -> 262 us  [per_device(): pl.pallas_call(functools.partial(layer_kernel, seq_count, exp_count, tail...]
    unnamed x15 -> x4, local copies, waits for them, and re-layouts: 3.17 us -> 6.46 us
where the time goes in v1:
time: 273 us; the launch traced here: 269 us
  Pallas kernels  262 us (96%)
  local copies, waits for them, and re-layouts  6.46 us (2%)
    pallas_call x1, Pallas kernels, per_device(): pl.pallas_call(functools.partial(layer_kernel, seq_count, exp_count, tail...  262 us
    unnamed x4, local copies, waits for them, and re-layouts  6.46 us

profile of v1, /device:TPU:25, one launch (start us, length us, event | category | flops | bytes accessed | tf_op | source)
XLA Modules:
  0.0 268.7 jit_solution(690179191014710737)
XLA Ops:
  0.0 1.4 copy.12.pairs_ref
  1.4 1.4 copy.13.ids_ref
  2.8 1.4 copy.14.gate_weight_ref
  4.2 262.2 %layer.1 = bf16[128,4096]{1,0:T(8,128)(2,1)} custom-call(s32[16,2]{1,0:T(8,128)} %copy.12.pairs_ref, s32[128,2]{1,0:T(8,128)} %copy.13.ids_ref, f32[128,2]{1,0:T(8,128)} %copy.14.gate_weight_ref, f32[1,4096]{1,0:T(1,128)} %bitcast.1, bf16[128,4096]{1,0:T(8,128)(2,1)} %in_hbm.1, bf16[128,4096]{1,0:T(8,128)(2,1)} %q_hbm.1, bf16[128,4096]{1,0:T(8,128)(2,1)} %k_hbm.1, ...), custom_call_target="tpu_custom_call" | custom-call | tf_op jit(solution)/shard_map/layer/pallas_call | solution.py:596
  266.4 2.3 copy.16

commit v2 on v1

--- a/solution.py
+++ b/solution.py
@@ -14,6 +14,7 @@
 DIST = 2
 OUTER = 2
 CORES = 2
+PARTS = 4
 
 very_negative = -1e30
 norm_epsilon = 1e-05
@@ -57,6 +58,69 @@
 
 def wide(value):
     return value.astype(jnp.float32)
+
+
+EIGHT_ORDER = ((0, 0), (2, 0), (1, 0), (3, 0), (3, 1), (1, 1), (2, 1), (0, 1))
+EIGHT_STEPS = (
+    ("V", 0), ("q", 0), ("a", (0, 0)), ("a", (0, 1)), ("a", (0, 2)), ("a", (0, 3)), ("m", 0), ("t", 0), ("q",
+    1), ("x", (0, 4)), ("x", (0, 5)), ("x", (0, 2)), ("x", (0, 3)), ("x", (0, 6)), ("x", (0, 1)), ("a", (1,
+    0)), ("a", (1, 1)), ("x", (0, 7)), ("a", (1, 2)), ("g", 0), ("g", 1), ("r", 0), ("a", (1, 3)), ("r", 1),
+    ("g", 2), ("m", 1), ("x", (1, 2)), ("g", 3), ("c", 0), ("h", (0, 0)), ("h", (0, 1)), ("x", (1, 3)), ("r",
+    2), ("h", (0, 2)), ("h", (0, 3)), ("x", (1, 1)), ("r", 3), ("x", (1, 7)), ("s", 0), ("x", (1, 6)), ("d",
+    (0, 0)), ("d", (0, 1)), ("f", 0), ("f", 1), ("c", 1), ("A", 0), ("x", (1, 4)), ("h", (1, 0)), ("x", (1,
+    5)), ("h", (1, 1)), ("g", 4), ("h", (1, 2)), ("g", 5), ("h", (1, 3)), ("r", 4), ("r", 5), ("B", 0), ("A",
+    1), ("s", 1), ("g", 6), ("d", (1, 0)), ("d", (1, 1)), ("c", 2), ("h", (2, 0)), ("h", (2, 1)), ("h", (2,
+    2)), ("h", (2, 3)), ("f", 2), ("s", 2), ("f", 3), ("r", 6), ("d", (2, 0)), ("g", 7), ("B", 1), ("A", 2),
+    ("d", (2, 1)), ("r", 7), ("B", 2), ("c", 3), ("f", 4), ("h", (3, 0)), ("A", 3), ("A", 4), ("f", 5), ("h",
+    (3, 1)), ("B", 3), ("h", (3, 2)), ("h", (3, 3)), ("s", 3), ("d", (3, 0)), ("d", (3, 1)), ("B", 4), ("A",
+    5), ("f", 6), ("A", 6), ("f", 7), ("B", 5), ("B", 6), ("A", 7), ("B", 7),
+)
+
+
+def plan(count, together, tiles):
+    if (count, together, tiles) == (8, 2, 4):
+        return EIGHT_ORDER, EIGHT_STEPS
+    chips, groups = count // CORES, count // together
+    order = [(j, p) for p in range(CORES) for j in range(chips)]
+    steps = [("V", 0), ("q", 0)] + [("a", (0, i)) for i in range(PARTS)] + [("t", 0), ("m", 0), ("q", 1)]
+    steps += [("a", (1, i)) for i in range(PARTS)] + [("m", 1)]
+    steps += [("x", (p, k)) for p in range(CORES) for k in range(1, count)]
+    ahead = together + 1
+    gathered, passed = 0, 0
+
+    def gather_to(last):
+        nonlocal gathered, passed
+        found = []
+        while gathered <= min(last, count - 1):
+            found.append(("g", gathered))
+            gathered += 1
+            if gathered > 1:
+                found.append(("r", passed))
+                passed += 1
+        if last >= count and passed < count:
+            found.append(("r", passed))
+            passed += 1
+        return found
+
+    steps += gather_to(ahead)
+    for p in range(groups):
+        base = p * together
+        steps.append(("c", p))
+        for n in range(tiles):
+            steps.append(("h", (p, n)))
+            steps += gather_to(base + ahead + ((n + 1) * together + tiles - 1) // tiles)
+        steps.append(("s", p))
+        for part in range(2):
+            steps.append(("d", (p, part)))
+            for k in range(part * together // 2, (part + 1) * together // 2):
+                if base > 0:
+                    steps.append(("A", base - together + k))
+                if base - together + k > 0:
+                    steps.append(("B", base - together + k - 1))
+        steps += [("f", base + i) for i in range(together)]
+    for k in range((groups - 1) * together, count):
+        steps += [("A", k), ("B", k - 1)]
+    return order, steps + [("B", count - 1)]
 
 
 def layer_kernel(
@@ -168,45 +232,39 @@
     wanted = [(first_block + i, first_block + i - (DIST - j)) for i in range(blocks) for j in range(slots)]
 
     def seen(p, found):
-        query, key = pairs_ref[p, 0], pairs_ref[p, 1]
+        query, key = pairs_ref[0, p], pairs_ref[1, p]
         return tuple(
             f + jnp.where((query == w[0]) & (key == w[1]), 1, 0) for f, w in zip(found, wanted)
         )
 
-    found = lax.fori_loop(0, pairs_ref.shape[0], seen, (jnp.int32(0),) * len(wanted))
+    found = lax.fori_loop(0, pairs_ref.shape[1], seen, (jnp.int32(0),) * len(wanted))
     for i in range(blocks):
         for j in range(slots):
             present[i, j] = found[i * slots + j]
 
     places = exp_count * capacity
-    named = [ids_ref[:, t : t + 1] for t in range(TOP)]
-    ranks = lax.broadcasted_iota(jnp.int32, (rows, HSZ), 1)
+    named = [ids_ref[t : t + 1, :] for t in range(TOP)]
+    ranks = lax.broadcasted_iota(jnp.int32, (HSZ, rows), 0)
     marks = [jnp.where(n == ranks, 1.0, 0.0) for n in named]
     earlier = jnp.where(
-        lax.broadcasted_iota(jnp.int32, (rows, rows), 1) < lax.broadcasted_iota(jnp.int32, (rows, rows), 0),
+        lax.broadcasted_iota(jnp.int32, (rows, rows), 0) < lax.broadcasted_iota(jnp.int32, (rows, rows), 1),
         1.0, 0.0,
     ).astype(jnp.bfloat16)
-    ahead = jnp.dot(earlier, sum(marks).astype(jnp.bfloat16), preferred_element_type=jnp.float32)
-    slot_ids = lax.broadcasted_iota(jnp.int32, (rows, places), 1)
-    choose = jnp.zeros((rows, places), jnp.float32)
-    weight = jnp.zeros((rows, places), jnp.float32)
+    ahead = jnp.dot(sum(marks).astype(jnp.bfloat16), earlier, preferred_element_type=jnp.float32)
+    slot_ids = lax.broadcasted_iota(jnp.int32, (places, rows), 0)
+    choose = jnp.zeros((places, rows), jnp.float32)
+    weight = jnp.zeros((places, rows), jnp.float32)
     for t in range(TOP):
-        position = jnp.sum(ahead * marks[t], axis=1, keepdims=True)
+        position = jnp.sum(ahead * marks[t], axis=0, keepdims=True)
         spot = named[t] * capacity + position.astype(jnp.int32) == slot_ids
         choose = jnp.where(spot, 1.0, choose)
-        weight = jnp.where(spot, gate_weight_ref[:, t : t + 1], weight)
+        weight = jnp.where(spot, gate_weight_ref[t : t + 1, :], weight)
     choose_ref[...] = choose.astype(jnp.bfloat16)
+    weight = weight.T
     coarse = weight.astype(jnp.bfloat16)
     coarse_ref[...] = coarse
     fine_ref[...] = (weight - coarse.astype(jnp.float32)).astype(jnp.bfloat16)
 
-    for i in range(2):
-        keep(i).wait()
-        relay(i, 0, "start")
-        for k in range(1, exp_count):
-            taken(i, k)
-            relay(i, k, "start")
-    keep(2).wait()
 
     def queries_of(parity):
         for j in range(chips):
@@ -216,16 +274,23 @@
             else:
                 taken(2, k)
 
-    queries_of(0)
-
-    @pl.when(c > 0)
-    def _():
-        for k in range(1, exp_count):
-            give(2, k).start()
-
-    for i in range(2):
-        for k in range(exp_count):
-            relay(i, k, "recv")
+    def late_queries():
+        @pl.when(c > 0)
+        def _():
+            for k in range(1, exp_count):
+                give(2, k).start()
+
+    def keys_and_values():
+        for i in range(2):
+            keep(i).wait()
+            relay(i, 0, "start")
+            for k in range(1, exp_count):
+                taken(i, k)
+                relay(i, k, "start")
+        keep(2).wait()
+        for i in range(2):
+            for k in range(exp_count):
+                relay(i, k, "recv")
 
     scale = 1.0 / math.sqrt(HSZ)
 
@@ -247,7 +312,7 @@
 
     part = BLK // CORES
 
-    def attend(parity):
+    def attend(parity, begin, end):
         def step(i):
             head = lax.rem(i, heads)
             block = lax.rem(lax.div(e, owners) + 1 + lax.div(i, heads), blocks)
@@ -286,18 +351,36 @@
                 def _():
                     own(head).start()
 
-        loop(0, blocks * heads, step)
+        loop(begin, end, step)
 
     def mixed(where):
         return wide(x_in[:, where]) + wide(attended[:, where])
 
-    def chunk(t):
-        return CORES * xor(z, lax.rem(t, chips), chips) + lax.div(t, chips)
+    order, program = plan(exp_count, together, hid_ref.shape[1] // tile)
+
+    def apart(k):
+        j, p = order[k]
+        return CORES * j + lax.rem(c + p, CORES)
+
+    def chunk(k):
+        j, p = order[k]
+        return CORES * xor(z, j, chips) + p
+
+    def here(k, act):
+        j, p = order[k]
+        if j == 0:
+            pl.when(c == p)(act)
+
+    def away(k, act):
+        j, p = order[k]
+        if j == 0:
+            pl.when(c != p)(act)
+        else:
+            act()
 
     def spread(k):
         d = xor(e, k, exp_count)
-        step = c * chips + lax.div(k, CORES)
-        return remote(outgoing.at[d], buf.at[a, b, e], z_send.at[k], z_recv.at[step], (s, d))
+        return remote(outgoing.at[d], buf.at[a, b, e], z_send.at[k], z_recv.at[k], (s, d))
 
     def stays():
         return pltpu.make_async_copy(outgoing.at[e], buf.at[a, b, e], local_sem)
@@ -328,20 +411,12 @@
         def normed_tile(n):
             where = pl.ds(pl.multiple_of(n * norm_tile, norm_tile), norm_tile)
             normed = (mixed(where) * factor * gain_ref[:, where]).astype(jnp.bfloat16)
-            picked = lax.dot_general(
-                choose_ref[...], normed, (((0,), (0,)), ((), ())), preferred_element_type=jnp.float32
-            )
+            picked = jnp.dot(choose_ref[...], normed, preferred_element_type=jnp.float32)
             outgoing[:, :, where] = picked.astype(outgoing.dtype).reshape(exp_count, capacity, norm_tile)
 
         loop(0, width // norm_tile, normed_tile)
         stays().start()
-        loop(1, exp_count, lambda k: spread(k).start())
-
-    attend(0)
-    pl.when(c == 0)(dispatch)
-    queries_of(1)
-    attend(1)
-    pl.when(c > 0)(dispatch)
+
 
     def directs(k):
         block = buf.at[a, b, chunk(k)]
@@ -360,29 +435,19 @@
             copies.append(remote(block, block, d_send.at[1, j, k], d_recv.at[1, j, k], outer))
         return copies
 
-    def gather_step(k):
-        @pl.when(k < exp_count)
-        def _():
-            @pl.when(k != c * chips)
-            def _():
-                arrived(buf.at[a, b, chunk(k)], z_send.at[k], z_recv.at[k])
-
-            @pl.when(k == c * chips)
-            def _():
-                stays().wait()
-
-            for copy in directs(k):
-                copy.start()
-
-        @pl.when((k > 0) & (k <= exp_count))
-        def _():
-            n = k - 1
-            m = chunk(n)
-            arrived(buf.at[other, b, m], x_send.at[0, n], x_recv.at[0, n])
-            for j in range(inner_count - 1):
-                arrived(buf.at[a, back[j], m], x_send.at[1 + j, n], x_recv.at[1 + j, n])
-            for copy in relays(n):
-                copy.start()
+    def gather(k):
+        away(k, lambda: arrived(buf.at[a, b, chunk(k)], z_send.at[apart(k)], z_recv.at[apart(k)]))
+        here(k, lambda: stays().wait())
+        for copy in directs(k):
+            copy.start()
+
+    def pass_on(k):
+        m = chunk(k)
+        arrived(buf.at[other, b, m], x_send.at[0, k], x_recv.at[0, k])
+        for j in range(inner_count - 1):
+            arrived(buf.at[a, back[j], m], x_send.at[1 + j, k], x_recv.at[1 + j, k])
+        for copy in relays(k):
+            copy.start()
 
     def complete(k):
         n = chunk(k)
@@ -408,12 +473,10 @@
         ]
 
     def third(k):
-        d = chunk(k)
-        where = xor(e, d, exp_count)
-        return remote(done.at[k], got.at[e], g_send.at[k], g_recv.at[where], (s, d))
-
-    def stay():
-        return pltpu.make_async_copy(done.at[c * chips], got.at[e], stay_sem)
+        return remote(done.at[k], got.at[e], g_send.at[k], g_recv.at[apart(k)], (s, chunk(k)))
+
+    def stay(k):
+        return pltpu.make_async_copy(done.at[k], got.at[e], stay_sem)
 
     def inner_sum(k, side):
         total = wide(buf[side, b, chunk(k), :, low])
@@ -424,87 +487,89 @@
     def outer_sum(k, lane):
         return wide(buf[a, lane, chunk(k), :, high]) + wide(in1[k, lane])
 
-    def sum_step(k):
-        @pl.when((k >= 0) & (k < exp_count))
-        def _():
-            sends = second(k)
-            for j in range(inner_count - 1):
-                arrived(in0.at[j, k], p_send.at[1 + j, k], p_recv.at[1 + j, k])
-            out0[k] = inner_sum(k, other).astype(out0.dtype)
-            sends[0].start()
-            arrived(in1.at[k], p_send.at[0, k], p_recv.at[0, k])
-            for j, f in enumerate(forth):
-                out1[j, k] = outer_sum(k, f).astype(out1.dtype)
-                sends[1 + j].start()
-
-        @pl.when((k > 0) & (k <= exp_count))
-        def _():
-            n = k - 1
-            arrived(mid0.at[n], m_send.at[0, n], m_recv.at[0, n])
-            done[n, :, low] = (inner_sum(n, a) + wide(mid0[n])).astype(done.dtype)
-            total = outer_sum(n, b)
-            for j in range(inner_count - 1):
-                arrived(mid1.at[j, n], m_send.at[1 + j, n], m_recv.at[1 + j, n])
-                total = total + wide(mid1[j, n])
-            done[n, :, high] = total.astype(done.dtype)
-
-            @pl.when(n == c * chips)
-            def _():
-                stay().start()
-
-            @pl.when(n != c * chips)
-            def _():
-                third(n).start()
-
-    loop(0, together + 2, gather_step)
-    for copy in weights:
-        copy.wait()
+    def half_sum(k):
+        sends = second(k)
+        for j in range(inner_count - 1):
+            arrived(in0.at[j, k], p_send.at[1 + j, k], p_recv.at[1 + j, k])
+        out0[k] = inner_sum(k, other).astype(out0.dtype)
+        sends[0].start()
+        arrived(in1.at[k], p_send.at[0, k], p_recv.at[0, k])
+        for j, f in enumerate(forth):
+            out1[j, k] = outer_sum(k, f).astype(out1.dtype)
+            sends[1 + j].start()
+
+    def whole_sum(k):
+        arrived(mid0.at[k], m_send.at[0, k], m_recv.at[0, k])
+        done[k, :, low] = (inner_sum(k, a) + wide(mid0[k])).astype(done.dtype)
+        total = outer_sum(k, b)
+        for j in range(inner_count - 1):
+            arrived(mid1.at[j, k], m_send.at[1 + j, k], m_recv.at[1 + j, k])
+            total = total + wide(mid1[j, k])
+        done[k, :, high] = total.astype(done.dtype)
+        here(k, lambda: stay(k).start())
+        away(k, lambda: third(k).start())
+
     tiles, wide_tiles = hid_ref.shape[1] // tile, width // wide_tile
-    stride, wide_stride = max(1, tiles // together), max(1, wide_tiles // together)
-
-    def expert_group(p):
-        base = p * together
+
+    def collect(p):
         for i in range(together):
-            complete(base + i)
-            x_ref[pl.ds(i * chunk_rows, chunk_rows)] = buf[:, :, chunk(base + i)].reshape(chunk_rows, width)
-
-        def hidden_tile(n):
-            where = pl.ds(pl.multiple_of(n * tile, tile), tile)
-            x = x_ref[...]
-            gate = jnp.dot(x, gate_ref[:, where], preferred_element_type=jnp.float32)
-            up = jnp.dot(x, up_ref[:, where], preferred_element_type=jnp.float32)
-            hid_ref[:, where] = (jax.nn.silu(gate) * up).astype(hid_ref.dtype)
-
-            @pl.when(lax.rem(n, stride) == 0)
-            def _():
-                gather_step(base + together + 2 + lax.div(n, stride))
-
-        loop(0, tiles, hidden_tile)
+            k = p * together + i
+            complete(k)
+            x_ref[pl.ds(i * chunk_rows, chunk_rows)] = buf[:, :, chunk(k)].reshape(chunk_rows, width)
+
+    def hidden_tile(n):
+        where = pl.ds(n * tile, tile)
+        x = x_ref[...]
+        gate = jnp.dot(x, gate_ref[:, where], preferred_element_type=jnp.float32)
+        up = jnp.dot(x, up_ref[:, where], preferred_element_type=jnp.float32)
+        hid_ref[:, where] = (jax.nn.silu(gate) * up).astype(hid_ref.dtype)
+
+    def gone(p):
         for i in range(together):
-            for copy in directs(base + i) + relays(base + i):
+            for copy in directs(p * together + i) + relays(p * together + i):
                 copy.wait_send()
 
+    def down_tiles(p, begin, end):
         def down_tile(n):
             where = pl.ds(pl.multiple_of(n * wide_tile, wide_tile), wide_tile)
             y = jnp.dot(hid_ref[...], down_ref[:, where], preferred_element_type=jnp.float32).astype(buf.dtype)
             for i in range(together):
-                buf[:, :, chunk(base + i), :, where] = y[i * chunk_rows : (i + 1) * chunk_rows].reshape(
-                    OUTER, inner_count, capacity, wide_tile
-                )
-
-            @pl.when(lax.rem(n, wide_stride) == 0)
-            def _():
-                sum_step(base - together + lax.div(n, wide_stride))
-
-        loop(0, wide_tiles, down_tile)
-        for i in range(together):
-            for copy in first(base + i):
-                copy.start()
-
-    loop(0, groups, expert_group)
-    loop((groups - 1) * together, exp_count + 1, sum_step)
-
-    stay().wait()
+                buf[:, :, chunk(p * together + i), :, where] = y[
+                    i * chunk_rows : (i + 1) * chunk_rows
+                ].reshape(OUTER, inner_count, capacity, wide_tile)
+
+        loop(begin, end, down_tile)
+
+    def leave(k):
+        for copy in first(k):
+            copy.start()
+
+    items = blocks * heads
+    acts = {
+        "V": lambda k: keys_and_values(),
+        "q": queries_of,
+        "t": lambda k: late_queries(),
+        "a": lambda k: attend(k[0], k[1] * items // PARTS, (k[1] + 1) * items // PARTS),
+        "m": lambda k: pl.when(c == k)(dispatch),
+        "x": lambda k: pl.when(c == k[0])(lambda: spread(k[1]).start()),
+        "g": gather,
+        "r": pass_on,
+        "c": collect,
+        "h": lambda k: hidden_tile(k[1]),
+        "s": gone,
+        "d": lambda k: down_tiles(k[0], k[1] * wide_tiles // 2, (k[1] + 1) * wide_tiles // 2),
+        "f": leave,
+        "A": half_sum,
+        "B": whole_sum,
+    }
+    for name, k in program:
+        if name == "c" and k == 0:
+            for copy in weights:
+                copy.wait()
+        acts[name](k)
+
+    for k in range(exp_count):
+        here(k, lambda: stay(k).wait())
     for k in range(1, exp_count):
         arrived(got.at[xor(e, k, exp_count)], g_send.at[k], g_recv.at[k])
 
@@ -525,21 +590,17 @@
         for k in range(1, exp_count):
             give(i, k).wait_send()
 
-    def finish(k):
+    for k in range(exp_count):
         for copy in first(k) + second(k):
             copy.wait_send()
-
-        @pl.when(k > 0)
-        def _():
-            spread(k).wait_send()
-            for head in range(heads):
-                send(xor(e, k, exp_count), head).wait_send()
-
-        @pl.when(k != c * chips)
-        def _():
-            third(k).wait_send()
-
-    loop(0, exp_count, finish)
+        away(k, lambda: third(k).wait_send())
+
+    def finish(k):
+        spread(k).wait_send()
+        for head in range(heads):
+            send(xor(e, k, exp_count), head).wait_send()
+
+    loop(1, exp_count, finish)
 
 
 def per_device(
@@ -570,7 +631,7 @@
         (rows, width),
         (exp_count, capacity, width),
         (exp_count, capacity, width),
-        (rows, places),
+        (places, rows),
         (rows, places),
         (rows, places),
         w_gate.shape[1:],
@@ -609,7 +670,7 @@
         ),
         name="layer",
     )(
-        pairs, expert_ids, gate_weights, norm_gain.reshape(1, width), inputs, queries, keys, values,
+        pairs.T, expert_ids.T, gate_weights.T, norm_gain.reshape(1, width), inputs, queries, keys, values,
         w_gate, w_up, w_down,
     )
 

time: 273 us -> 257 us (0.941); the launches traced: 269 us -> 257 us
  Pallas kernels: 262 us -> 255 us
  local copies, waits for them, and re-layouts: 6.46 us -> 2.29 us
    pallas_call x1, Pallas kernels: 262 us -> 255 us  [per_device(): pl.pallas_call(functools.partial(layer_kernel, seq_count, exp_count, tail...]
    unnamed x4 -> x1, local copies, waits for them, and re-layouts: 6.46 us -> 2.29 us
where the time goes in v2:
time: 257 us
  Pallas kernels  255 us (99%)
    pallas_call x1, Pallas kernels, per_device(): pl.pallas_call(functools.partial(layer_kernel, seq_count, exp_count, tail...  255 us

profile of v2, /device:TPU:25, one launch (start us, length us, event | category | flops | bytes accessed | tf_op | source)
XLA Modules:
  0.0 257.2 jit_solution(2999127485703130163)
XLA Ops:
  0.0 254.9 %layer.1 = bf16[128,4096]{1,0:T(8,128)(2,1)} custom-call(s32[2,16]{1,0:T(2,128)} %bitcast.5, s32[2,128]{1,0:T(2,128)} %bitcast.6, f32[2,128]{1,0:T(2,128)} %bitcast.7, f32[1,4096]{1,0:T(1,128)} %bitcast.4, bf16[128,4096]{1,0:T(8,128)(2,1)} %in_hbm.1, bf16[128,4096]{1,0:T(8,128)(2,1)} %q_hbm.1, bf16[128,4096]{1,0:T(8,128)(2,1)} %k_hbm.1, ...), custom_call_target="tpu_custom_call" | custom-call | tf_op jit(solution)/shard_map/layer/pallas_call | solution.py:657
  255.0 2.3 copy.13

commit v3 on v2

--- a/solution.py
+++ b/solution.py
@@ -60,20 +60,20 @@
     return value.astype(jnp.float32)
 
 
-EIGHT_ORDER = ((0, 0), (2, 0), (1, 0), (3, 0), (3, 1), (1, 1), (2, 1), (0, 1))
+EIGHT_ORDER = ((0, 0), (1, 0), (3, 0), (2, 0), (3, 1), (2, 1), (1, 1), (0, 1))
 EIGHT_STEPS = (
-    ("V", 0), ("q", 0), ("a", (0, 0)), ("a", (0, 1)), ("a", (0, 2)), ("a", (0, 3)), ("m", 0), ("t", 0), ("q",
-    1), ("x", (0, 4)), ("x", (0, 5)), ("x", (0, 2)), ("x", (0, 3)), ("x", (0, 6)), ("x", (0, 1)), ("a", (1,
-    0)), ("a", (1, 1)), ("x", (0, 7)), ("a", (1, 2)), ("g", 0), ("g", 1), ("r", 0), ("a", (1, 3)), ("r", 1),
-    ("g", 2), ("m", 1), ("x", (1, 2)), ("g", 3), ("c", 0), ("h", (0, 0)), ("h", (0, 1)), ("x", (1, 3)), ("r",
-    2), ("h", (0, 2)), ("h", (0, 3)), ("x", (1, 1)), ("r", 3), ("x", (1, 7)), ("s", 0), ("x", (1, 6)), ("d",
-    (0, 0)), ("d", (0, 1)), ("f", 0), ("f", 1), ("c", 1), ("A", 0), ("x", (1, 4)), ("h", (1, 0)), ("x", (1,
-    5)), ("h", (1, 1)), ("g", 4), ("h", (1, 2)), ("g", 5), ("h", (1, 3)), ("r", 4), ("r", 5), ("B", 0), ("A",
-    1), ("s", 1), ("g", 6), ("d", (1, 0)), ("d", (1, 1)), ("c", 2), ("h", (2, 0)), ("h", (2, 1)), ("h", (2,
-    2)), ("h", (2, 3)), ("f", 2), ("s", 2), ("f", 3), ("r", 6), ("d", (2, 0)), ("g", 7), ("B", 1), ("A", 2),
-    ("d", (2, 1)), ("r", 7), ("B", 2), ("c", 3), ("f", 4), ("h", (3, 0)), ("A", 3), ("A", 4), ("f", 5), ("h",
-    (3, 1)), ("B", 3), ("h", (3, 2)), ("h", (3, 3)), ("s", 3), ("d", (3, 0)), ("d", (3, 1)), ("B", 4), ("A",
-    5), ("f", 6), ("A", 6), ("f", 7), ("B", 5), ("B", 6), ("A", 7), ("B", 7),
+    ("V", 0), ("q", 0), ("a", (0, 0)), ("a", (0, 1)), ("a", (0, 2)), ("a", (0, 3)), ("m", 0), ("x", (0, 1)),
+    ("x", (0, 2)), ("t", 0), ("x", (0, 3)), ("x", (0, 6)), ("x", (0, 7)), ("x", (0, 4)), ("x", (0, 5)), ("g",
+    0), ("g", 1), ("r", 0), ("r", 1), ("c", 0), ("q", 1), ("h", (0, 0)), ("h", (0, 1)), ("g", 2), ("h", (0,
+    2)), ("h", (0, 3)), ("g", 3), ("a", (1, 0)), ("r", 2), ("s", 0), ("a", (1, 1)), ("d", (0, 0)), ("r", 3),
+    ("a", (1, 2)), ("d", (0, 1)), ("f", 0), ("f", 1), ("a", (1, 3)), ("c", 1), ("h", (1, 0)), ("A", 0), ("m",
+    1), ("x", (1, 6)), ("h", (1, 1)), ("x", (1, 1)), ("h", (1, 2)), ("h", (1, 3)), ("x", (1, 7)), ("A", 1),
+    ("s", 1), ("d", (1, 0)), ("x", (1, 2)), ("d", (1, 1)), ("x", (1, 5)), ("x", (1, 4)), ("f", 2), ("B", 0),
+    ("f", 3), ("A", 2), ("x", (1, 3)), ("g", 4), ("B", 1), ("g", 5), ("r", 4), ("r", 5), ("g", 6), ("c", 2),
+    ("B", 2), ("g", 7), ("h", (2, 0)), ("h", (2, 1)), ("h", (2, 2)), ("r", 6), ("h", (2, 3)), ("s", 2), ("r",
+    7), ("d", (2, 0)), ("d", (2, 1)), ("A", 3), ("f", 4), ("c", 3), ("B", 3), ("h", (3, 0)), ("h", (3, 1)),
+    ("A", 4), ("f", 5), ("h", (3, 2)), ("h", (3, 3)), ("B", 4), ("s", 3), ("d", (3, 0)), ("d", (3, 1)), ("f",
+    6), ("A", 5), ("A", 6), ("f", 7), ("B", 5), ("B", 6), ("A", 7), ("B", 7),
 )
 
 

time: 257 us -> 239 us (0.930); the launches traced: 257 us -> 236 us
  Pallas kernels: 255 us -> 234 us
    pallas_call x1, Pallas kernels: 255 us -> 234 us  [per_device(): pl.pallas_call(functools.partial(layer_kernel, seq_count, exp_count, tail...]
where the time goes in v3:
time: 239 us; the launch traced here: 236 us
  Pallas kernels  234 us (98%)
    pallas_call x1, Pallas kernels, per_device(): pl.pallas_call(functools.partial(layer_kernel, seq_count, exp_count, tail...  234 us

profile of v3, /device:TPU:25, one launch (start us, length us, event | category | flops | bytes accessed | tf_op | source)
XLA Modules:
  0.0 236.2 jit_solution(15155286068056423685)
XLA Ops:
  0.0 233.9 %layer.1 = bf16[128,4096]{1,0:T(8,128)(2,1)} custom-call(s32[2,16]{1,0:T(2,128)} %bitcast.5, s32[2,128]{1,0:T(2,128)} %bitcast.6, f32[2,128]{1,0:T(2,128)} %bitcast.7, f32[1,4096]{1,0:T(1,128)} %bitcast.4, bf16[128,4096]{1,0:T(8,128)(2,1)} %in_hbm.1, bf16[128,4096]{1,0:T(8,128)(2,1)} %q_hbm.1, bf16[128,4096]{1,0:T(8,128)(2,1)} %k_hbm.1, ...), custom_call_target="tpu_custom_call" | custom-call | tf_op jit(solution)/shard_map/layer/pallas_call | solution.py:657
  233.9 2.3 copy.13

commit v4 on v3

--- a/solution.py
+++ b/solution.py
@@ -62,18 +62,20 @@
 
 EIGHT_ORDER = ((0, 0), (1, 0), (3, 0), (2, 0), (3, 1), (2, 1), (1, 1), (0, 1))
 EIGHT_STEPS = (
-    ("V", 0), ("q", 0), ("a", (0, 0)), ("a", (0, 1)), ("a", (0, 2)), ("a", (0, 3)), ("m", 0), ("x", (0, 1)),
-    ("x", (0, 2)), ("t", 0), ("x", (0, 3)), ("x", (0, 6)), ("x", (0, 7)), ("x", (0, 4)), ("x", (0, 5)), ("g",
-    0), ("g", 1), ("r", 0), ("r", 1), ("c", 0), ("q", 1), ("h", (0, 0)), ("h", (0, 1)), ("g", 2), ("h", (0,
-    2)), ("h", (0, 3)), ("g", 3), ("a", (1, 0)), ("r", 2), ("s", 0), ("a", (1, 1)), ("d", (0, 0)), ("r", 3),
-    ("a", (1, 2)), ("d", (0, 1)), ("f", 0), ("f", 1), ("a", (1, 3)), ("c", 1), ("h", (1, 0)), ("A", 0), ("m",
-    1), ("x", (1, 6)), ("h", (1, 1)), ("x", (1, 1)), ("h", (1, 2)), ("h", (1, 3)), ("x", (1, 7)), ("A", 1),
-    ("s", 1), ("d", (1, 0)), ("x", (1, 2)), ("d", (1, 1)), ("x", (1, 5)), ("x", (1, 4)), ("f", 2), ("B", 0),
-    ("f", 3), ("A", 2), ("x", (1, 3)), ("g", 4), ("B", 1), ("g", 5), ("r", 4), ("r", 5), ("g", 6), ("c", 2),
-    ("B", 2), ("g", 7), ("h", (2, 0)), ("h", (2, 1)), ("h", (2, 2)), ("r", 6), ("h", (2, 3)), ("s", 2), ("r",
-    7), ("d", (2, 0)), ("d", (2, 1)), ("A", 3), ("f", 4), ("c", 3), ("B", 3), ("h", (3, 0)), ("h", (3, 1)),
-    ("A", 4), ("f", 5), ("h", (3, 2)), ("h", (3, 3)), ("B", 4), ("s", 3), ("d", (3, 0)), ("d", (3, 1)), ("f",
-    6), ("A", 5), ("A", 6), ("f", 7), ("B", 5), ("B", 6), ("A", 7), ("B", 7),
+    ("V", 0), ("q", 0), ("a", (0, 0)), ("a", (0, 1)), ("a", (0, 2)), ("a", (0, 3)), ("m", 0), ("t", 0), ("x",
+    (0, 2)), ("x", (0, 3)), ("x", (0, 6)), ("x", (0, 1)), ("x", (0, 7)), ("x", (0, 4)), ("x", (0, 5)), ("g",
+    0), ("g", 1), ("R", 0), ("r", 0), ("r", 1), ("R", 1), ("c", 0), ("q", 1), ("h", (0, 0)), ("h", (0, 1)),
+    ("g", 2), ("h", (0, 2)), ("h", (0, 3)), ("s", 0), ("g", 3), ("d", (0, 0)), ("a", (1, 0)), ("d", (0, 1)),
+    ("r", 2), ("R", 2), ("R", 3), ("r", 3), ("F", 0), ("f", 0), ("F", 1), ("a", (1, 1)), ("a", (1, 2)), ("a",
+    (1, 3)), ("c", 1), ("f", 1), ("h", (1, 0)), ("A", 0), ("h", (1, 1)), ("E", 0), ("h", (1, 2)), ("m", 1),
+    ("x", (1, 7)), ("x", (1, 1)), ("h", (1, 3)), ("x", (1, 6)), ("x", (1, 3)), ("s", 1), ("d", (1, 0)), ("x",
+    (1, 5)), ("f", 2), ("A", 1), ("x", (1, 4)), ("d", (1, 1)), ("F", 2), ("E", 1), ("f", 3), ("B", 0), ("F",
+    3), ("E", 2), ("x", (1, 2)), ("A", 2), ("g", 4), ("R", 4), ("g", 5), ("B", 1), ("g", 6), ("r", 4), ("R",
+    5), ("B", 2), ("r", 5), ("c", 2), ("g", 7), ("E", 3), ("R", 6), ("A", 3), ("h", (2, 0)), ("h", (2, 1)),
+    ("r", 6), ("h", (2, 2)), ("R", 7), ("r", 7), ("h", (2, 3)), ("s", 2), ("d", (2, 0)), ("f", 4), ("d", (2,
+    1)), ("F", 4), ("B", 3), ("c", 3), ("h", (3, 0)), ("h", (3, 1)), ("E", 4), ("f", 5), ("A", 4), ("h", (3,
+    2)), ("F", 5), ("h", (3, 3)), ("s", 3), ("B", 4), ("d", (3, 0)), ("d", (3, 1)), ("f", 6), ("F", 6), ("A",
+    5), ("E", 5), ("E", 6), ("A", 6), ("B", 5), ("f", 7), ("F", 7), ("B", 6), ("A", 7), ("E", 7), ("B", 7),
 )
 
 
@@ -120,7 +122,9 @@
         steps += [("f", base + i) for i in range(together)]
     for k in range((groups - 1) * together, count):
         steps += [("A", k), ("B", k - 1)]
-    return order, steps + [("B", count - 1)]
+    steps += [("B", count - 1)]
+    pairs = {"r": "rR", "f": "Ff", "A": "AE"}
+    return order, [(name, k) for step, k in steps for name in pairs.get(step, step)]
 
 
 def layer_kernel(
@@ -131,7 +135,7 @@
     gate_ref, up_ref, down_ref, buf, x_ref, hid_ref, in0, in1, out0, out1, mid0, mid1, done,
     in_sem, own_sem, q_send, q_recv, f_send, f_recv, a_own, a_send, a_recv,
     local_sem, stay_sem, w_sem, z_send, z_recv, x_send, x_recv, d_send, d_recv,
-    p_send, p_recv, m_send, m_recv, g_send, g_recv,
+    p_send, p_recv, m_send, m_recv, g_send, g_recv, put_sem,
 ):
     s, e = lax.axis_index("seq"), lax.axis_index("exp")
     z, c = lax.div(e, CORES), lax.rem(e, CORES)
@@ -441,12 +445,15 @@
         for copy in directs(k):
             copy.start()
 
-    def pass_on(k):
-        m = chunk(k)
-        arrived(buf.at[other, b, m], x_send.at[0, k], x_recv.at[0, k])
+    def pass_low(k):
+        arrived(buf.at[other, b, chunk(k)], x_send.at[0, k], x_recv.at[0, k])
+        for copy in relays(k)[0::2]:
+            copy.start()
+
+    def pass_high(k):
         for j in range(inner_count - 1):
-            arrived(buf.at[a, back[j], m], x_send.at[1 + j, k], x_recv.at[1 + j, k])
-        for copy in relays(k):
+            arrived(buf.at[a, back[j], chunk(k)], x_send.at[1 + j, k], x_recv.at[1 + j, k])
+        for copy in relays(k)[1::2]:
             copy.start()
 
     def complete(k):
@@ -487,16 +494,17 @@
     def outer_sum(k, lane):
         return wide(buf[a, lane, chunk(k), :, high]) + wide(in1[k, lane])
 
-    def half_sum(k):
-        sends = second(k)
+    def low_sum(k):
         for j in range(inner_count - 1):
             arrived(in0.at[j, k], p_send.at[1 + j, k], p_recv.at[1 + j, k])
         out0[k] = inner_sum(k, other).astype(out0.dtype)
-        sends[0].start()
+        second(k)[0].start()
+
+    def high_sum(k):
         arrived(in1.at[k], p_send.at[0, k], p_recv.at[0, k])
         for j, f in enumerate(forth):
             out1[j, k] = outer_sum(k, f).astype(out1.dtype)
-            sends[1 + j].start()
+            second(k)[1 + j].start()
 
     def whole_sum(k):
         arrived(mid0.at[k], m_send.at[0, k], m_recv.at[0, k])
@@ -540,9 +548,12 @@
 
         loop(begin, end, down_tile)
 
-    def leave(k):
-        for copy in first(k):
+    def leave_low(k):
+        for copy in first(k)[1:]:
             copy.start()
+
+    def leave_high(k):
+        first(k)[0].start()
 
     items = blocks * heads
     acts = {
@@ -553,13 +564,16 @@
         "m": lambda k: pl.when(c == k)(dispatch),
         "x": lambda k: pl.when(c == k[0])(lambda: spread(k[1]).start()),
         "g": gather,
-        "r": pass_on,
+        "r": pass_low,
+        "R": pass_high,
         "c": collect,
         "h": lambda k: hidden_tile(k[1]),
         "s": gone,
         "d": lambda k: down_tiles(k[0], k[1] * wide_tiles // 2, (k[1] + 1) * wide_tiles // 2),
-        "f": leave,
-        "A": half_sum,
+        "f": leave_low,
+        "F": leave_high,
+        "A": low_sum,
+        "E": high_sum,
         "B": whole_sum,
     }
     for name, k in program:
@@ -573,13 +587,18 @@
     for k in range(1, exp_count):
         arrived(got.at[xor(e, k, exp_count)], g_send.at[k], g_recv.at[k])
 
+    def put(n):
+        where = pl.ds(pl.multiple_of(n * norm_tile, norm_tile), norm_tile)
+        return pltpu.make_async_copy(x_in.at[:, where], out_ref.at[:, where], put_sem.at[n])
+
     def final_tile(n):
         where = pl.ds(pl.multiple_of(n * norm_tile, norm_tile), norm_tile)
         flat = got[:, :, where].reshape(places, norm_tile)
         combined = jnp.dot(coarse_ref[...], flat, preferred_element_type=jnp.float32) + jnp.dot(
             fine_ref[...], flat, preferred_element_type=jnp.float32
         )
-        out_ref[:, where] = (mixed(where) + combined).astype(out_ref.dtype)
+        x_in[:, where] = (mixed(where) + combined).astype(x_in.dtype)
+        put(n).start()
 
     loop(0, width // norm_tile, final_tile)
 
@@ -601,6 +620,7 @@
             send(xor(e, k, exp_count), head).wait_send()
 
     loop(1, exp_count, finish)
+    loop(0, width // norm_tile, lambda n: put(n).wait())
 
 
 def per_device(
@@ -658,13 +678,14 @@
         functools.partial(layer_kernel, seq_count, exp_count, tail, together, tile, wide_tile, norm_tile),
         out_shape=jax.ShapeDtypeStruct((rows, width), kind),
         in_specs=[pl.BlockSpec(memory_space=pltpu.SMEM)] + [HELD] * 3 + [ANY] * 7,
-        out_specs=HELD,
+        out_specs=ANY,
         scratch_shapes=[pltpu.SMEM((blocks, DIST + 1), jnp.int32)]
         + [pltpu.VMEM(shape, kind) for shape in vmem]
         + [DMA, DMA((3,))]
         + [DMA(shape) for shape in sems]
         + [DMA, DMA, DMA((3,))]
-        + [DMA(shape) for shape in more],
+        + [DMA(shape) for shape in more]
+        + [DMA((width // norm_tile,))],
         compiler_params=pltpu.CompilerParams(
             collective_id=1, has_side_effects=True, vmem_limit_bytes=67043328
         ),

time: 239 us -> 239 us (level)
  no operation moved by 1% of the time
where the time goes in v4:
time: 239 us; the launch traced here: 235 us
  Pallas kernels  233 us (97%)
    pallas_call x1, Pallas kernels, per_device(): pl.pallas_call(functools.partial(layer_kernel, seq_count, exp_count, tail...  233 us

profile of v4, /device:TPU:25, one launch (start us, length us, event | category | flops | bytes accessed | tf_op | source)
XLA Modules:
  0.0 235.2 jit_solution(18299607891704152389)
XLA Ops:
  0.0 232.9 %layer.1 = bf16[128,4096]{1,0:T(8,128)(2,1)} custom-call(s32[2,16]{1,0:T(2,128)} %bitcast.5, s32[2,128]{1,0:T(2,128)} %bitcast.6, f32[2,128]{1,0:T(2,128)} %bitcast.7, f32[1,4096]{1,0:T(1,128)} %bitcast.4, bf16[128,4096]{1,0:T(8,128)(2,1)} %in_hbm.1, bf16[128,4096]{1,0:T(8,128)(2,1)} %q_hbm.1, bf16[128,4096]{1,0:T(8,128)(2,1)} %k_hbm.1, ...), custom_call_target="tpu_custom_call" | custom-call | tf_op jit(solution)/shard_map/layer/pallas_call | solution.py:677
  232.9 2.3 copy.13
